TPU v7x, 32 devices: a whole 2x2x4 slice. The times are simulated.
32 devices in a mesh: groups: 2 (over y), cluster: 4 (over x, core), station: 4 (over z).
Axes of the slice: x: 2, y: 2, z: 4, core: 2. Of those that a mesh axis runs over, the one named last changes fastest.
Arguments:
- waveforms: float32 [256, 16, 3, 256], P(('groups', 'cluster'), 'station'), parts along dimension 0, may hold values from -120 to 120
- event_mask: int32 [256, 16], P(('groups', 'cluster'), 'station'), parts along dimension 0, may hold values 0 or 1
- station_weight: float32 [32], P('groups'), parts along dimension 0, may hold values from 0.01 to 10
- partners: int32 [4, 8], P(None, 'groups'), parts along dimension 1, may hold values from 0 to 3, as said below
- pair_list: int32 [4, 8, 256, 2], P(None, ('groups', 'cluster')), parts along dimension 1, may hold values from 0 to 31
- counts: int32 [8], P('groups'), parts along dimension 0, may hold values from 16 to 32, as said below
Outputs:
- stacked: float32 [4, 8, 256, 512], P(None, ('groups', 'cluster'), 'station'), parts along dimension 1
There are 2 independent parts, one for each index of `groups`. A program takes and returns all parts, laid end to end along the dimension named above; each array names one. Nothing has to cross between parts.
Inputs may be any that keep to these rules, and one draw needn't show every extreme that they name: `partners`: in every round each cluster is paired with itself or with one of its two neighbours on the cluster cycle (index plus or minus one, modulo 4), and the pairing is mutual. `counts`: event slots of a cluster at or above its count are padding. Every draw has a cluster holding 32 events and another holding 32 // 2.
All inputs are finite; a program needn't handle non-finite values. No bound on the sum of `event_mask` on one device may be relied on, other than what follows from the above.
Results may differ from a plain program's by a relative error of at most 0.0003.
Values sent between devices are 32-bit elements; how exact they have to be, the bound alone decides.
A program may use at most 64 MiB of HBM per device.

v0:
```python
import math

import jax
import jax.numpy as jnp
from jax import lax
from jax.sharding import PartitionSpec as P

epsilon = 1e-06
HIGHEST = lax.Precision.HIGHEST


def passed_along(array, axis, by):
    length = lax.axis_size(axis)
    return lax.ppermute(array, axis, [(i, (i + by) % length) for i in range(length)])


def make_tables(seismogram_readings):
    record_duration = 2 * seismogram_readings
    time_points = jnp.arange(seismogram_readings, dtype=jnp.int32)
    rotation_radians = time_points[:, None] * time_points[None, :] % record_duration
    angles = rotation_radians.astype(jnp.float32) * (math.pi / seismogram_readings)
    forward = jnp.concatenate([jnp.cos(angles), -jnp.sin(angles)], axis=1)
    column = jnp.arange(record_duration, dtype=jnp.int32)
    delayed_seismograms = (column + seismogram_readings) % record_duration
    backward_rotation_radians = (
        time_points[:, None] * delayed_seismograms[None, :] % record_duration
    )
    angles_back = backward_rotation_radians.astype(jnp.float32) * (math.pi / seismogram_readings)
    normalizing_multiplier = (
        jnp.where(time_points == 0, 1.0, 2.0).astype(jnp.float32)[:, None] / record_duration
    )
    inverse = jnp.concatenate(
        [
            normalizing_multiplier * jnp.cos(angles_back),
            -normalizing_multiplier * jnp.sin(angles_back),
        ],
        axis=0,
    )
    return (forward, inverse)


def normalized(waveforms, event_mask):
    energy = jnp.sum(waveforms * waveforms, axis=-1, keepdims=True)
    scaled = waveforms * lax.rsqrt(energy + epsilon)
    return scaled * event_mask[:, :, None, None].astype(jnp.float32)


def transform(traces, forward):
    events, stations, channels, seismogram_readings = traces.shape
    flattened = traces.reshape(events * stations * channels, seismogram_readings)
    spectra = jnp.dot(flattened, forward, precision=HIGHEST, preferred_element_type=jnp.float32)
    return spectra.reshape(events, stations * channels, 2 * seismogram_readings)


def cross_block(own_side, other_side, first_index, second):
    half_width = own_side.shape[-1] // 2
    left_rows = jnp.take(own_side, first_index, axis=0)
    right_rows = jnp.take(other_side, second, axis=0)
    real_part = jnp.sum(
        left_rows[..., :half_width] * right_rows[..., :half_width]
        + left_rows[..., half_width:] * right_rows[..., half_width:],
        axis=1,
    )
    imag_part = jnp.sum(
        left_rows[..., half_width:] * right_rows[..., :half_width]
        - left_rows[..., :half_width] * right_rows[..., half_width:],
        axis=1,
    )
    return jnp.concatenate([real_part, imag_part], axis=-1)


def pair_spectra(own_side, other_side, pairs_now, valid_pairs):
    pair_count = pairs_now.shape[0]
    block_rows = math.gcd(pair_count, 64)
    firsts = pairs_now[:, 0].reshape(pair_count // block_rows, block_rows)
    seconds = pairs_now[:, 1].reshape(pair_count // block_rows, block_rows)

    def one_block(indices):
        return cross_block(own_side, other_side, indices[0], indices[1])

    stacked_rows = lax.map(one_block, (firsts, seconds)).reshape(pair_count, own_side.shape[-1])
    return stacked_rows * valid_pairs[:, None]


def on_device(waveforms, event_mask, station_weight, partners, pair_list, counts):
    events, stations, channels, seismogram_readings = waveforms.shape
    rounds_total = partners.shape[0]
    forward, inverse = make_tables(seismogram_readings)
    cluster_here = lax.axis_index("cluster")
    cluster_width = lax.axis_size("cluster")
    station_here = lax.axis_index("station")
    local_weight = lax.dynamic_slice_in_dim(station_weight, station_here * stations, stations)
    network_scale = 1.0 / (channels * jnp.sum(station_weight))
    unit_traces = normalized(waveforms, event_mask)
    own_spectra = transform(unit_traces, forward)
    weight_rows = jnp.repeat(local_weight, channels)
    weighted = own_spectra * weight_rows[None, :, None]
    partner_ids = partners[:, cluster_here]
    right_neighbour = (cluster_here + 1) % cluster_width
    traces_from_left = passed_along(unit_traces, "cluster", 1)
    traces_from_right = passed_along(unit_traces, "cluster", -1)
    both_sides = transform(jnp.concatenate([traces_from_left, traces_from_right], axis=0), forward)
    from_left = both_sides[:events]
    from_right = both_sides[events:]
    shares = []
    for turn_index in range(rounds_total):
        partner_now = partner_ids[turn_index]
        other_side = jnp.where(
            partner_now == cluster_here,
            own_spectra,
            jnp.where(partner_now == right_neighbour, from_right, from_left),
        )
        pairs_now = pair_list[turn_index, 0]
        own_count = counts[cluster_here]
        other_count = counts[partner_now]
        valid_pairs = ((pairs_now[:, 0] < own_count) & (pairs_now[:, 1] < other_count)).astype(
            jnp.float32
        )
        partial_value = pair_spectra(weighted, other_side, pairs_now, valid_pairs)
        shares.append(lax.psum_scatter(partial_value, "station", scatter_dimension=0, tiled=True))
    summed = jnp.stack(shares)
    share_rows = summed.shape[1]
    result = jnp.dot(
        summed.reshape(rounds_total * share_rows, 2 * seismogram_readings),
        inverse,
        precision=HIGHEST,
        preferred_element_type=jnp.float32,
    )
    return (result * network_scale).reshape(rounds_total, 1, share_rows, 2 * seismogram_readings)


def solution(mesh):
    return jax.shard_map(
        on_device,
        mesh=mesh,
        in_specs=(
            P(("groups", "cluster"), "station", None, None),
            P(("groups", "cluster"), "station"),
            P("groups"),
            P(None, "groups"),
            P(None, ("groups", "cluster"), None, None),
            P("groups"),
        ),
        out_specs=P(None, ("groups", "cluster"), "station", None),
        check_vma=False,
    )
```

profile of v0, /device:TPU:0, one launch (start us, length us, event | category | flops | bytes accessed | tf_op | source)
XLA Modules:
  0.0 267.5 jit_solution(18406320838458610675)
XLA Ops:
  10.3 2.0 collective-permute-start.1
  22.7 1.9 and_convert_fusion.2
  32.2 1.9 and_convert_fusion
  39.6 2.2 select_n.164
  41.8 5.9 %copy_select_fusion.3 = (f32[32,12,512]{2,0,1:T(8,128)S(1)}, f32[32,12,512]{2,0,1:T(8,128)}, f32[32,12,512]{2,0,1:T(8,128)}, f32[32,12,512]{2,0,1:T(8,128)}, f32[32,12,512]{2,0,1:T(8,128)S(1)}) fusion(f32[32,12,512]{2,1,0:T(8,128)S(1)} %select_n.146, pred[]{:T(512)S(6)} %eq.47, f32[32,12,512]{2,1,0:T(8,128)} %select_n.164, pred[]{:T(512)S(6)} %eq.53, ...), kind=kOutput, calls=%fused_computation.80 | convolution fusion | flops 605093888 | bytes 7995444 | tf_op jit(solution)/shard_map/dot_general | solution.py:51
  50.5 41.5 %while.40 = (s32[]{:T(128)}, f32[4,64,512]{2,1,0:T(8,128)}, s32[4,64]{1,0:T(4,128)S(1)}, f32[32,12,512]{2,1,0:T(8,128)S(1)}, s32[4,64]{1,0:T(4,128)S(1)}, /*index=5*/f32[32,12,512]{2,1,0:T(8,128)}, s32[]{:T(128)}) while((s32[]{:T(128)}, f32[4,64,512]{2,1,0:T(8,128)}, s32[4,64]{1,0:T(4,128)S(1)}, f32[32,12,512]{2,1,0:T(8,128)S(1)}, ...), condition=%wide.region_4.6_spmd, body=%wide.region_1.5_spmd.sunk | while | flops 2362114 | bytes 16132945 | solution.py:81
  50.5 2.0 gather_fusion.1
  52.6 1.8 broadcast_select_fusion.17
  54.4 3.3 %gather_fusion = f32[64,12,512]{2,1,0:T(8,128)} fusion(f32[32,12,512]{2,1,0:T(8,128)} %get-tuple-element.636, s32[1024]{0:T(1024)S(1)} %pad_clamp_fusion.16), kind=kCustom, calls=%fused_computation.1.clone.clone.1 | custom fusion | bytes 3145984 | tf_op jit(solution)/shard_map/while/body/eval_jaxpr/jit(_take)/gather | solution.py:58
  60.9 2.0 gather_fusion.1
  64.7 3.3 %gather_fusion = f32[64,12,512]{2,1,0:T(8,128)} fusion(f32[32,12,512]{2,1,0:T(8,128)} %get-tuple-element.636, s32[1024]{0:T(1024)S(1)} %pad_clamp_fusion.16), kind=kCustom, calls=%fused_computation.1.clone.clone.1 | custom fusion | bytes 3145984 | tf_op jit(solution)/shard_map/while/body/eval_jaxpr/jit(_take)/gather | solution.py:58
  71.3 2.0 gather_fusion.1
  73.3 1.8 broadcast_select_fusion.17
  75.1 3.3 %gather_fusion = f32[64,12,512]{2,1,0:T(8,128)} fusion(f32[32,12,512]{2,1,0:T(8,128)} %get-tuple-element.636, s32[1024]{0:T(1024)S(1)} %pad_clamp_fusion.16), kind=kCustom, calls=%fused_computation.1.clone.clone.1 | custom fusion | bytes 3145984 | tf_op jit(solution)/shard_map/while/body/eval_jaxpr/jit(_take)/gather | solution.py:58
  81.6 2.0 gather_fusion.1
  83.7 1.8 broadcast_select_fusion.17
  85.5 3.3 %gather_fusion = f32[64,12,512]{2,1,0:T(8,128)} fusion(f32[32,12,512]{2,1,0:T(8,128)} %get-tuple-element.636, s32[1024]{0:T(1024)S(1)} %pad_clamp_fusion.16), kind=kCustom, calls=%fused_computation.1.clone.clone.1 | custom fusion | bytes 3145984 | tf_op jit(solution)/shard_map/while/body/eval_jaxpr/jit(_take)/gather | solution.py:58
  92.0 2.0 bitcast_multiply_fusion.3
  96.6 41.5 %while.41 = (s32[]{:T(128)}, f32[4,64,512]{2,1,0:T(8,128)}, s32[4,64]{1,0:T(4,128)S(1)}, f32[32,12,512]{2,1,0:T(8,128)S(1)}, s32[4,64]{1,0:T(4,128)S(1)}, /*index=5*/f32[32,12,512]{2,1,0:T(8,128)}, s32[]{:T(128)}) while((s32[]{:T(128)}, f32[4,64,512]{2,1,0:T(8,128)}, s32[4,64]{1,0:T(4,128)S(1)}, f32[32,12,512]{2,1,0:T(8,128)S(1)}, ...), condition=%wide.region_9.11_spmd, body=%wide.region_6.10_spmd.sunk | while | flops 2362114 | bytes 16132945 | solution.py:81
  96.6 2.0 gather_fusion.3
  98.6 1.8 broadcast_select_fusion.19
  100.5 3.3 %gather_fusion.2 = f32[64,12,512]{2,1,0:T(8,128)} fusion(f32[32,12,512]{2,1,0:T(8,128)} %get-tuple-element.615, s32[1024]{0:T(1024)S(1)} %pad_clamp_fusion.18), kind=kCustom, calls=%fused_computation.3.clone.clone.1 | custom fusion | bytes 3145984 | tf_op jit(solution)/shard_map/while/body/eval_jaxpr/jit(_take)/gather | solution.py:58
  107.0 2.0 gather_fusion.3
  109.0 1.8 broadcast_select_fusion.19
  110.8 3.3 %gather_fusion.2 = f32[64,12,512]{2,1,0:T(8,128)} fusion(f32[32,12,512]{2,1,0:T(8,128)} %get-tuple-element.615, s32[1024]{0:T(1024)S(1)} %pad_clamp_fusion.18), kind=kCustom, calls=%fused_computation.3.clone.clone.1 | custom fusion | bytes 3145984 | tf_op jit(solution)/shard_map/while/body/eval_jaxpr/jit(_take)/gather | solution.py:58
  117.4 2.0 gather_fusion.3
  119.4 1.8 broadcast_select_fusion.19
  121.2 3.3 %gather_fusion.2 = f32[64,12,512]{2,1,0:T(8,128)} fusion(f32[32,12,512]{2,1,0:T(8,128)} %get-tuple-element.615, s32[1024]{0:T(1024)S(1)} %pad_clamp_fusion.18), kind=kCustom, calls=%fused_computation.3.clone.clone.1 | custom fusion | bytes 3145984 | tf_op jit(solution)/shard_map/while/body/eval_jaxpr/jit(_take)/gather | solution.py:58
  127.7 2.0 gather_fusion.3
  129.8 1.8 broadcast_select_fusion.19
  131.6 3.3 %gather_fusion.2 = f32[64,12,512]{2,1,0:T(8,128)} fusion(f32[32,12,512]{2,1,0:T(8,128)} %get-tuple-element.615, s32[1024]{0:T(1024)S(1)} %pad_clamp_fusion.18), kind=kCustom, calls=%fused_computation.3.clone.clone.1 | custom fusion | bytes 3145984 | tf_op jit(solution)/shard_map/while/body/eval_jaxpr/jit(_take)/gather | solution.py:58
  138.1 2.6 copy.60
  140.7 1.9 bitcast_multiply_fusion.2
  143.5 41.5 %while.42 = (s32[]{:T(128)}, f32[4,64,512]{2,1,0:T(8,128)}, s32[4,64]{1,0:T(4,128)S(1)}, f32[32,12,512]{2,1,0:T(8,128)S(1)}, s32[4,64]{1,0:T(4,128)S(1)}, /*index=5*/f32[32,12,512]{2,1,0:T(8,128)}, s32[]{:T(128)}) while((s32[]{:T(128)}, f32[4,64,512]{2,1,0:T(8,128)}, s32[4,64]{1,0:T(4,128)S(1)}, f32[32,12,512]{2,1,0:T(8,128)S(1)}, ...), condition=%wide.region_14.16_spmd, body=%wide.region_11.15_spmd.sunk | while | flops 2362114 | bytes 16132945 | solution.py:81
  143.6 2.0 gather_fusion.5
  145.6 1.8 broadcast_select_fusion.21
  147.4 3.3 %gather_fusion.4 = f32[64,12,512]{2,1,0:T(8,128)} fusion(f32[32,12,512]{2,1,0:T(8,128)} %get-tuple-element.594, s32[1024]{0:T(1024)S(1)} %pad_clamp_fusion.20), kind=kCustom, calls=%fused_computation.5.clone.clone.1 | custom fusion | bytes 3145984 | tf_op jit(solution)/shard_map/while/body/eval_jaxpr/jit(_take)/gather | solution.py:58
  150.7 1.8 broadcast_select_fusion.20
  153.9 2.0 gather_fusion.5
  156.0 1.8 broadcast_select_fusion.21
  157.8 3.3 %gather_fusion.4 = f32[64,12,512]{2,1,0:T(8,128)} fusion(f32[32,12,512]{2,1,0:T(8,128)} %get-tuple-element.594, s32[1024]{0:T(1024)S(1)} %pad_clamp_fusion.20), kind=kCustom, calls=%fused_computation.5.clone.clone.1 | custom fusion | bytes 3145984 | tf_op jit(solution)/shard_map/while/body/eval_jaxpr/jit(_take)/gather | solution.py:58
  164.3 2.0 gather_fusion.5
  166.4 1.8 broadcast_select_fusion.21
  168.2 3.3 %gather_fusion.4 = f32[64,12,512]{2,1,0:T(8,128)} fusion(f32[32,12,512]{2,1,0:T(8,128)} %get-tuple-element.594, s32[1024]{0:T(1024)S(1)} %pad_clamp_fusion.20), kind=kCustom, calls=%fused_computation.5.clone.clone.1 | custom fusion | bytes 3145984 | tf_op jit(solution)/shard_map/while/body/eval_jaxpr/jit(_take)/gather | solution.py:58
  174.7 2.0 gather_fusion.5
  178.5 3.3 %gather_fusion.4 = f32[64,12,512]{2,1,0:T(8,128)} fusion(f32[32,12,512]{2,1,0:T(8,128)} %get-tuple-element.594, s32[1024]{0:T(1024)S(1)} %pad_clamp_fusion.20), kind=kCustom, calls=%fused_computation.5.clone.clone.1 | custom fusion | bytes 3145984 | tf_op jit(solution)/shard_map/while/body/eval_jaxpr/jit(_take)/gather | solution.py:58
  185.0 2.6 copy.63
  187.6 1.9 bitcast_multiply_fusion.1
  190.5 41.5 %while.43 = (s32[]{:T(128)}, f32[4,64,512]{2,1,0:T(8,128)}, s32[4,64]{1,0:T(4,128)S(1)}, f32[32,12,512]{2,1,0:T(8,128)S(1)}, s32[4,64]{1,0:T(4,128)S(1)}, /*index=5*/f32[32,12,512]{2,1,0:T(8,128)}, s32[]{:T(128)}) while((s32[]{:T(128)}, f32[4,64,512]{2,1,0:T(8,128)}, s32[4,64]{1,0:T(4,128)S(1)}, f32[32,12,512]{2,1,0:T(8,128)S(1)}, ...), condition=%wide.region_19.21_spmd, body=%wide.region_16.20_spmd.sunk | while | flops 2362114 | bytes 16132945 | solution.py:81
  190.5 2.0 gather_fusion.7
  194.4 3.3 %gather_fusion.6 = f32[64,12,512]{2,1,0:T(8,128)} fusion(f32[32,12,512]{2,1,0:T(8,128)} %get-tuple-element.573, s32[1024]{0:T(1024)S(1)} %pad_clamp_fusion.22), kind=kCustom, calls=%fused_computation.7.clone.clone.1 | custom fusion | bytes 3145984 | tf_op jit(solution)/shard_map/while/body/eval_jaxpr/jit(_take)/gather | solution.py:58
  197.6 1.8 broadcast_select_fusion.22
  200.9 2.0 gather_fusion.7
  202.9 1.8 broadcast_select_fusion.23
  204.8 3.3 %gather_fusion.6 = f32[64,12,512]{2,1,0:T(8,128)} fusion(f32[32,12,512]{2,1,0:T(8,128)} %get-tuple-element.573, s32[1024]{0:T(1024)S(1)} %pad_clamp_fusion.22), kind=kCustom, calls=%fused_computation.7.clone.clone.1 | custom fusion | bytes 3145984 | tf_op jit(solution)/shard_map/while/body/eval_jaxpr/jit(_take)/gather | solution.py:58
  211.3 2.0 gather_fusion.7
  213.3 1.8 broadcast_select_fusion.23
  215.1 3.3 %gather_fusion.6 = f32[64,12,512]{2,1,0:T(8,128)} fusion(f32[32,12,512]{2,1,0:T(8,128)} %get-tuple-element.573, s32[1024]{0:T(1024)S(1)} %pad_clamp_fusion.22), kind=kCustom, calls=%fused_computation.7.clone.clone.1 | custom fusion | bytes 3145984 | tf_op jit(solution)/shard_map/while/body/eval_jaxpr/jit(_take)/gather | solution.py:58
  221.7 2.0 gather_fusion.7
  225.5 3.3 %gather_fusion.6 = f32[64,12,512]{2,1,0:T(8,128)} fusion(f32[32,12,512]{2,1,0:T(8,128)} %get-tuple-element.573, s32[1024]{0:T(1024)S(1)} %pad_clamp_fusion.22), kind=kCustom, calls=%fused_computation.7.clone.clone.1 | custom fusion | bytes 3145984 | tf_op jit(solution)/shard_map/while/body/eval_jaxpr/jit(_take)/gather | solution.py:58
  232.0 1.9 bitcast_multiply_fusion
  235.3 2.1 cosine_multiply_fusion
  237.5 20.5 %reduce-scatter.11.cloned.1.call-done = f32[64,512]{1,0:T(8,128)} async-done(((f32[256,512]{1,0:T(8,128)}), f32[64,512]{1,0:T(8,128)}) %reduce-scatter.11.cloned.1.call-update) | async-done | bytes 131088 | tf_op jit(solution)/shard_map/reduce_scatter | solution.py:120
  259.1 1.8 convolution_multiply_fusion
  (165 shorter events, 79.0 us)
Async XLA Ops:
  6.5 5.7 %copy-start = (s32[4,4]{1,0:T(4,128)S(1)}, s32[4,4]{1,0:T(4,128)}, u32[]{:S(2)}) copy-start(s32[4,4]{1,0:T(4,128)} %param.19) | copy-start | bytes 196
  6.5 230.9 %reduce-scatter.5.cloned.1.call-start = ((), (), s32[]{:S(2)}) async-start(), calls=%async_computation.4 | async-start | bytes 655360 | tf_op jit(solution)/shard_map/reduce_scatter | solution.py:120
  9.7 25.5 %copy-start.3 = (f32[32,4,3,256]{3,0,2,1:T(8,128)}, f32[32,4,3,256]{3,0,2,1:T(8,128)S(1)}, u32[]{:S(2)}) copy-start(f32[32,4,3,256]{3,0,2,1:T(8,128)S(1)} %fusion.24) | copy-start | bytes 1179652
  9.7 24.5 %collective-permute-start = (f32[32,4,3,256]{3,0,2,1:T(8,128)S(1)}, f32[32,4,3,256]{3,0,2,1:T(8,128)S(1)}, u32[]{:S(2)}, u32[]{:S(2)}) collective-permute-start(f32[32,4,3,256]{3,0,2,1:T(8,128)S(1)} %fusion.24), channel_id=1, source_target_pairs={{0,4},{4,8},{8,12},{12,0},{1,5},{5,9},{9,13},{13,1},{2,6},{6,10},{... | collective-permute-start | bytes 1179656 | tf_op jit(solution)/shard_map/ppermute | solution.py:14
  10.3 23.9 %collective-permute-start.1 = (f32[32,4,3,256]{3,0,2,1:T(8,128)S(1)}, f32[32,4,3,256]{3,0,2,1:T(8,128)S(1)}, u32[]{:S(2)}, u32[]{:S(2)}) collective-permute-start(f32[32,4,3,256]{3,0,2,1:T(8,128)S(1)} %fusion.24), channel_id=1, source_target_pairs={{0,12},{4,0},{8,4},{12,8},{1,13},{5,1},{9,5},{13,9},{2,14},{6,2},{... | collective-permute-start | bytes 1179656 | tf_op jit(solution)/shard_map/ppermute | solution.py:14
  32.2 3.0 %copy-start.2 = (f32[256,256]{1,0:T(8,128)}, f32[256,256]{1,0:T(8,128)S(1)}, u32[]{:S(2)}) copy-start(f32[256,256]{1,0:T(8,128)S(1)} %get-tuple-element.355) | copy-start | bytes 786436
  92.0 2.3 copy-start.1
  94.0 143.4 %reduce-scatter.7.cloned.1.call-start = ((), (), s32[]{:S(2)}) async-start(), calls=%async_computation.5 | async-start | bytes 655360 | tf_op jit(solution)/shard_map/reduce_scatter | solution.py:120
  142.6 94.8 %reduce-scatter.9.cloned.1.call-start = ((), (), s32[]{:S(2)}) async-start(), calls=%async_computation.6 | async-start | bytes 655360 | tf_op jit(solution)/shard_map/reduce_scatter | solution.py:120
  189.6 68.4 %reduce-scatter.11.cloned.1.call-start = ((), (), s32[]{:S(2)}) async-start(), calls=%async_computation.7 | async-start | bytes 655360 | tf_op jit(solution)/shard_map/reduce_scatter | solution.py:120
  190.5 43.5 %copy-start.4 = (f32[16]{0:T(128)S(1)}, f32[16]{0:T(128)}, u32[]{:S(2)}) copy-start(f32[16]{0:T(128)} %param.18) | copy-start | bytes 196
Sparse Core Ops, SparseCore 0:
  94.2 23.8 reduce-scatter.4
  142.7 23.8 reduce-scatter.6
  189.7 23.9 reduce-scatter.8
  234.1 23.8 reduce-scatter.10
where the time goes:
time: 270 us; the launch traced here: 268 us
  local copies, waits for them, and re-layouts  106 us (39%)
  other arithmetic  102 us (38%)
  between operations  26.5 us (10%)
  waiting for transfers between devices  20.7 us (8%)
  matrix products  9.13 us (3%)
  starting transfers between devices  2.83 us (1%)
    gather x16, local copies, waits for them, and re-layouts, cross_block(): right_rows = jnp.take(other_side, second, axis=0)  52.1 us
    gather x16, local copies, waits for them, and re-layouts, cross_block(): left_rows = jnp.take(own_side, first_index, axis=0)  32.6 us
    select_n x16, other arithmetic, cross_block(): left_rows = jnp.take(own_side, first_index, axis=0)  28.8 us
    select_n x16, other arithmetic, cross_block(): right_rows = jnp.take(other_side, second, axis=0)  28.7 us
    reduce_scatter x4, waiting for transfers between devices, on_device(): lax.psum_scatter(partial_value, 'station', scatter_dimension=0, tiled=True)  20.6 us
    reduce_sum x16, other arithmetic, cross_block(): jnp.sum(left_rows[..., :half_width] * right_rows[..., :half_width] + left...  12 us
    mul x6, other arithmetic, pair_spectra(): return stacked_rows * valid_pairs[:, None]  11.7 us
    dynamic_update_slice x16, other arithmetic, pair_spectra(): lax.map(one_block, (firsts, seconds))  10.7 us
  transfers between devices with their start and end apart: 6, of which 1 were waited for; matrix products, arithmetic and copies ran while one was open for 56% of the time, Pallas kernels for 0%

commit v1 on v0

v1 whole, which is shorter than its diff:
```python
import functools
import math

import jax
import jax.numpy as jnp
import numpy as np
from jax import lax
from jax.experimental import pallas as pl
from jax.experimental.pallas import tpu as pltpu
from jax.sharding import PartitionSpec as P

epsilon = 1e-06
LANES = 128
MESH = pl.DeviceIdType.MESH


def split_table(table):
    high = table.astype(np.float32).astype(jnp.bfloat16)
    low = (table - high.astype(np.float64)).astype(np.float32).astype(jnp.bfloat16)
    return np.asarray(high), np.asarray(low)


def make_tables(samples):
    duration = 2 * samples
    time_points = np.arange(samples)
    angles = (time_points[:, None] * time_points[None, :] % duration) * (math.pi / samples)
    forward = np.concatenate([np.cos(angles), -np.sin(angles)], axis=1)
    lags = (np.arange(duration) + samples) % duration
    back = (time_points[:, None] * lags[None, :] % duration) * (math.pi / samples)
    scale = np.where(time_points == 0, 1.0, 2.0)[:, None] / duration
    inverse = np.concatenate([scale * np.cos(back), -scale * np.sin(back)], axis=0)
    return split_table(forward) + split_table(inverse)


def halves(x):
    high = x.astype(jnp.bfloat16)
    return high, (x - high.astype(jnp.float32)).astype(jnp.bfloat16)


def dot3(x, table_high, table_low):
    high, low = halves(x)
    dot = functools.partial(jnp.dot, preferred_element_type=jnp.float32)
    return dot(high, table_high) + (dot(high, table_low) + dot(low, table_high))


def kernel(sizes, first_ref, second_ref, weight_ref, traces_ref, scale_ref, fh_ref, fl_ref, gh_ref,
           gl_ref, out_ref, arrived, weighted, spectra, part, from_below, from_above,
           side_send, side_recv, up_send, up_recv, down_send, down_recv):
    events, rows, rounds, chain, share, ring, channels = sizes
    cols = fh_ref.shape[1] // LANES
    half = cols // 2
    lines = rows * cols
    cluster = lax.axis_index("cluster")
    here = lax.axis_index("station")
    right, left = lax.rem(cluster + 1, ring), lax.rem(cluster + ring - 1, ring)

    barrier = pltpu.get_barrier_semaphore()
    for side in (left, right):
        pl.semaphore_signal(barrier, inc=1, device_id={"cluster": side}, device_id_type=MESH)

    @pl.when(here > 0)
    def _():
        pl.semaphore_signal(barrier, inc=1, device_id={"station": here - 1}, device_id_type=MESH)

    @pl.when(here < chain - 1)
    def _():
        pl.semaphore_signal(barrier, inc=1, device_id={"station": here + 1}, device_id_type=MESH)

    pl.semaphore_wait(barrier, 2 + (here + chain - 1) // chain + (2 * chain - 2 - here) // chain)

    def to_side(slot, side):
        return pltpu.make_async_remote_copy(
            src_ref=traces_ref, dst_ref=arrived.at[slot], send_sem=side_send.at[slot],
            recv_sem=side_recv.at[slot], device_id={"cluster": side}, device_id_type=MESH)

    to_right, to_left = to_side(0, right), to_side(1, left)
    to_right.start()
    to_left.start()

    def place(values, row, base, ref):
        for col in range(cols):
            line = (col // half) * (lines // 2) + row * half + col % half
            start = base * lines + line
            flat = ref.reshape(ref.shape[0] * lines, LANES)
            flat[pl.ds(start, events, stride=lines), :] = values[:, col * LANES:(col + 1) * LANES]

    def transform(source, base, also_weighted):
        group = 4 if rows % 4 == 0 else 1
        for first in range(0, rows, group):
            found = dot3(source[pl.ds(first * events, group * events), :], fh_ref[...], fl_ref[...])
            for k in range(group):
                row = first + k
                values = found[k * events:(k + 1) * events]
                place(values, row, base * events, spectra)
                if also_weighted:
                    place(values * weight_ref[here * (rows // channels) + row // channels], row, 0, weighted)

    transform(traces_ref, 0, True)
    to_left.wait()
    transform(arrived.at[1], 2, False)
    to_right.wait()
    transform(arrived.at[0], 1, False)

    sub = lax.broadcasted_iota(jnp.int32, (8, LANES), 0)
    in_low4 = sub < 4
    in_low2 = (sub & 2) == 0

    def fold(x, y, lower, by):
        return jnp.where(lower, x, y) + pltpu.roll(jnp.where(lower, y, x), by, 0)

    deep = lines // 2

    def one_pair(spot):
        a = weighted[first_ref[spot]]
        b = spectra[second_ref[spot]]
        re_a, im_a, re_b, im_b = a[:deep], a[deep:], b[:deep], b[deep:]
        real = re_a * re_b + im_a * im_b
        imag = im_a * re_b - re_a * im_b
        return (sum(real[k:k + 8] for k in range(0, deep, 8)),
                sum(imag[k:k + 8] for k in range(0, deep, 8)))

    def fill(turn, dest):
        base = (turn * chain + dest) * share

        def body(step, carry):
            for k in range(0, 8, 2):
                spot = base + step * 8 + k
                real0, imag0 = one_pair(spot)
                real1, imag1 = one_pair(spot + 1)
                reals = fold(real0, real1, in_low4, 4)
                imags = fold(imag0, imag1, in_low4, 4)
                both = jnp.where(in_low2, reals, imags) + jnp.where(
                    in_low2, pltpu.roll(reals, 6, 0), pltpu.roll(imags, 2, 0))
                part[turn * chain + dest, pl.ds(pl.multiple_of(step * 32 + k * 4, 8), 8), :] = both
            return carry

        lax.fori_loop(0, share // 8, body, 0)

    def upward(turn, dest):
        spot = turn * chain + dest
        return pltpu.make_async_remote_copy(
            src_ref=part.at[spot], dst_ref=from_below.at[spot], send_sem=up_send.at[spot],
            recv_sem=up_recv.at[spot], device_id={"station": here + 1}, device_id_type=MESH)

    def downward(turn, dest):
        spot = turn * chain + dest
        return pltpu.make_async_remote_copy(
            src_ref=part.at[spot], dst_ref=from_above.at[spot], send_sem=down_send.at[spot],
            recv_sem=down_recv.at[spot], device_id={"station": here - 1}, device_id_type=MESH)

    far_first = sorted(range(chain), key=lambda d: -abs(2 * d - chain + 1))

    def compute(turn):
        for dest in far_first:
            fill(turn, dest)

            @pl.when((here == 0) & (dest > here))
            def _():
                upward(turn, dest).start()

            @pl.when((here == chain - 1) & (dest < here))
            def _():
                downward(turn, dest).start()

    def forward(turn):
        for dest in far_first:
            spot = turn * chain + dest

            @pl.when((here > 0) & (dest > here))
            def _():
                upward(turn, dest).wait_recv()
                part[spot] = part[spot] + from_below[spot]
                upward(turn, dest).start()

            @pl.when((here < chain - 1) & (dest < here))
            def _():
                downward(turn, dest).wait_recv()
                part[spot] = part[spot] + from_above[spot]
                downward(turn, dest).start()

        spot = turn * chain + here

        @pl.when(here > 0)
        def _():
            upward(turn, here).wait_recv()
            part[spot] = part[spot] + from_below[spot]

        @pl.when(here < chain - 1)
        def _():
            downward(turn, here).wait_recv()
            part[spot] = part[spot] + from_above[spot]

        total = jnp.zeros((share, gh_ref.shape[1]), jnp.float32)
        for col in range(cols):
            piece = part[spot, pl.ds(col, share, stride=cols), :]
            table = pl.ds(col * LANES, LANES)
            total = total + dot3(piece, gh_ref[table, :], gl_ref[table, :])
        out_ref[turn] = total * scale_ref[turn]

    compute(0)

    def turn_body(turn, carry):
        compute(turn + 1)
        forward(turn)
        return carry

    lax.fori_loop(0, rounds - 1, turn_body, 0)
    forward(rounds - 1)

    def drain(turn, carry):
        for dest in range(chain):
            @pl.when(dest > here)
            def _():
                upward(turn, dest).wait_send()

            @pl.when(dest < here)
            def _():
                downward(turn, dest).wait_send()
        return carry

    lax.fori_loop(0, rounds, drain, 0)


def on_device(waveforms, event_mask, station_weight, partners, pair_list, counts):
    events, stations, channels, samples = waveforms.shape
    rounds, _, pairs, _ = pair_list.shape
    cluster = lax.axis_index("cluster")
    ring = lax.axis_size("cluster")
    here = lax.axis_index("station")
    chain = lax.axis_size("station")
    rows = stations * channels
    share = pairs // chain
    cols = 2 * samples // LANES
    fh, fl, gh, gl = make_tables(samples)

    energy = jnp.sum(waveforms * waveforms, axis=-1, keepdims=True)
    unit = waveforms * (lax.rsqrt(energy + epsilon) * event_mask[:, :, None, None].astype(jnp.float32))
    traces = jnp.transpose(unit, (1, 2, 0, 3)).reshape(rows * events, samples)

    partner = partners[:, cluster]
    slot = jnp.where(partner == cluster, 0, jnp.where(partner == (cluster + 1) % ring, 2, 1))
    i, j = pair_list[:, 0, :, 0], pair_list[:, 0, :, 1]
    first = i.reshape(-1)
    second = (slot[:, None] * events + j).reshape(-1)
    valid = ((i < counts[cluster]) & (j < counts[partner][:, None])).astype(jnp.float32)
    scale = valid / (channels * jnp.sum(station_weight))
    scale = lax.dynamic_slice_in_dim(scale, here * share, share, 1)[:, :, None]

    vmem = pl.BlockSpec(memory_space=pltpu.VMEM)
    smem = pl.BlockSpec(memory_space=pltpu.SMEM)
    blocks = rounds * chain
    block = pltpu.VMEM((blocks, share * cols, LANES), jnp.float32)
    out = pl.pallas_call(
        functools.partial(kernel, (events, rows, rounds, chain, share, ring, channels)),
        out_shape=jax.ShapeDtypeStruct((rounds, share, 2 * samples), jnp.float32),
        in_specs=[smem, smem, smem] + [vmem] * 6,
        out_specs=vmem,
        scratch_shapes=[
            pltpu.VMEM((2, rows * events, samples), jnp.float32),
            pltpu.VMEM((events, rows * cols, LANES), jnp.float32),
            pltpu.VMEM((3 * events, rows * cols, LANES), jnp.float32),
            block, block, block,
            pltpu.SemaphoreType.DMA((2,)), pltpu.SemaphoreType.DMA((2,)),
            pltpu.SemaphoreType.DMA((blocks,)), pltpu.SemaphoreType.DMA((blocks,)),
            pltpu.SemaphoreType.DMA((blocks,)), pltpu.SemaphoreType.DMA((blocks,)),
        ],
        compiler_params=pltpu.CompilerParams(
            collective_id=0, has_side_effects=True, vmem_limit_bytes=40 << 20),
        name="stack_pairs",
    )(first, second, station_weight, traces, scale, fh, fl, gh, gl)
    return out[:, None]


def solution(mesh):
    return jax.shard_map(
        on_device,
        mesh=mesh,
        in_specs=(
            P(("groups", "cluster"), "station", None, None),
            P(("groups", "cluster"), "station"),
            P("groups"),
            P(None, "groups"),
            P(None, ("groups", "cluster"), None, None),
            P("groups"),
        ),
        out_specs=P(None, ("groups", "cluster"), "station", None),
        check_vma=False,
    )
```

time: 270 us -> 76.6 us (0.28)
  the two profiles are of different devices: /device:TPU:0 before, /device:TPU:14 now
where the time goes in v1:
time: 76.6 us; the launch traced here: 76.3 us
  Pallas kernels  68.2 us (89%)
  local copies, waits for them, and re-layouts  5.43 us (7%)
  other arithmetic  1.94 us (3%)
    pallas_call x1, Pallas kernels, on_device(): pl.pallas_call(functools.partial(kernel, (events, rows, rounds, chain, sh...  68.2 us
    unnamed x24, local copies, waits for them, and re-layouts  3.92 us

profile of v1, /device:TPU:14, one launch (start us, length us, event | category | flops | bytes accessed | tf_op | source)
XLA Modules:
  0.0 76.3 jit_solution(12902731047953946723)
XLA Ops:
  0.0 0.0 copy-start.5
  0.0 0.0 copy-start.9
  0.0 0.7 copy-done.5
  0.7 0.0 copy-start.8
  0.7 0.6 dynamic_slice.10
  1.2 0.0 copy-start.4
  1.2 0.0 copy-start.6
  1.2 0.7 copy-done.4
  1.9 0.6 reduce_sum.19
  3.1 0.0 copy-done.8
  3.1 0.2 fusion.1
  3.3 0.0 copy-done.9
  3.3 0.6 gather_fusion
  4.0 0.0 copy-start.7
  4.0 0.1 broadcast_bitcast_fusion
  4.0 0.6 copy-done.7
  4.7 0.7 fusion
  5.4 0.1 select_bitcast_fusion
  5.4 0.1 copy.16
  5.5 0.0 copy-done.6
  5.5 0.2 multiply_reduce_fusion
  5.8 0.1 copy.18.scale_ref
  5.9 0.0 copy-start.1
  5.9 0.0 copy-start.3
  5.9 0.2 multiply_bitcast_fusion
  6.1 0.0 copy-start
  6.1 0.0 copy-start.2
  6.1 0.1 copy.17
  6.2 0.7 copy-done.1
  6.9 0.1 copy-done.3
  7.0 0.2 copy-done
  7.2 0.1 copy-done.2
  7.3 68.2 %stack_pairs.1 = f32[4,64,512]{2,1,0:T(8,128)S(1)} custom-call(s32[1024]{0:T(1024)S(1)} %bitcast.21, s32[1024]{0:T(1024)S(1)} %add.48.second_ref, f32[16]{0:T(128)S(1)} %copy-done.4, f32[384,256]{1,0:T(8,128)S(1)} %bitcast.20, f32[4,64,1]{2,1,0:T(8,128)S(1)} %copy.18.scale_ref, bf16[256,512]{1,0:T(8,128)(2,1)S(1)} %copy-done.3, ...), custom_call_target="tpu_custom_call" | custom-call | tf_op jit(solution)/shard_map/stack_pairs/pallas_call | solution.py:253
  75.5 0.8 %copy.29 = f32[4,1,64,512]{3,2,1,0:T(8,128)} copy(f32[4,1,64,512]{3,2,1,0:T(8,128)S(1)} %bitcast.19) | data formatting | bytes 1048576
  (7 shorter events, 0.1 us)
Async XLA Ops:
  0.0 0.7 copy-start.5
  0.0 3.3 %copy-start.9 = (s32[32,4]{0,1:T(4,128)S(1)}, s32[32,4]{0,1:T(4,128)}, u32[]{:S(2)}) copy-start(s32[32,4]{0,1:T(4,128)} %param.11) | copy-start | bytes 1540
  0.7 2.4 %copy-start.8 = (s32[4,4]{1,0:T(4,128)S(1)}, s32[4,4]{1,0:T(4,128)}, u32[]{:S(2)}) copy-start(s32[4,4]{1,0:T(4,128)} %param.13) | copy-start | bytes 196
  1.2 0.7 copy-start.4
  1.2 4.3 %copy-start.6 = (f32[32,4,3,256]{3,1,2,0:T(4,128)S(1)}, f32[32,4,3,256]{3,1,2,0:T(4,128)}, u32[]{:S(2)}) copy-start(f32[32,4,3,256]{3,1,2,0:T(4,128)} %param.10) | copy-start | bytes 1179652
  4.0 0.7 copy-start.7
  5.9 1.0 %copy-start.1 = (bf16[512,512]{1,0:T(8,128)(2,1)S(1)}, bf16[512,512]{1,0:T(8,128)(2,1)}, u32[]{:S(2)}) copy-start(bf16[512,512]{1,0:T(8,128)(2,1)} %constant.52.clone.gh_ref) | copy-start | bytes 1572868
  5.9 1.1 %copy-start.3 = (bf16[256,512]{1,0:T(8,128)(2,1)S(1)}, bf16[256,512]{1,0:T(8,128)(2,1)}, u32[]{:S(2)}) copy-start(bf16[256,512]{1,0:T(8,128)(2,1)} %constant.50.clone.fh_ref) | copy-start | bytes 786436
  6.1 1.1 %copy-start = (bf16[512,512]{1,0:T(8,128)(2,1)S(1)}, bf16[512,512]{1,0:T(8,128)(2,1)}, u32[]{:S(2)}) copy-start(bf16[512,512]{1,0:T(8,128)(2,1)} %constant.53.clone.gl_ref) | copy-start | bytes 1572868
  6.1 1.2 %copy-start.2 = (bf16[256,512]{1,0:T(8,128)(2,1)S(1)}, bf16[256,512]{1,0:T(8,128)(2,1)}, u32[]{:S(2)}) copy-start(bf16[256,512]{1,0:T(8,128)(2,1)} %constant.51.clone.fl_ref) | copy-start | bytes 786436

commit v2 on v1

--- a/solution.py
+++ b/solution.py
@@ -43,9 +43,10 @@
     return dot(high, table_high) + (dot(high, table_low) + dot(low, table_high))
 
 
-def kernel(sizes, first_ref, second_ref, weight_ref, traces_ref, scale_ref, fh_ref, fl_ref, gh_ref,
-           gl_ref, out_ref, arrived, weighted, spectra, part, from_below, from_above,
-           side_send, side_recv, up_send, up_recv, down_send, down_recv):
+def kernel(sizes, pair_ref, partner_ref, count_ref, weight_ref, traces_ref, fh_hbm, fl_hbm, gh_hbm,
+           gl_hbm, out_ref, fh_ref, fl_ref, gh_ref, gl_ref, arrived, end_arrived, weighted,
+           spectra, end_weighted, end_spectra, part, from_below, from_above, table_sem, side_send,
+           side_recv, end_send, end_recv, up_send, up_recv, down_send, down_recv):
     events, rows, rounds, chain, share, ring, channels = sizes
     cols = fh_ref.shape[1] // LANES
     half = cols // 2
@@ -54,6 +55,14 @@
     here = lax.axis_index("station")
     right, left = lax.rem(cluster + 1, ring), lax.rem(cluster + ring - 1, ring)
 
+    tables = [
+        pltpu.make_async_copy(source, target, table_sem.at[k])
+        for k, (source, target) in enumerate(
+            ((fh_hbm, fh_ref), (fl_hbm, fl_ref), (gh_hbm, gh_ref), (gl_hbm, gl_ref)))
+    ]
+    for table in tables:
+        table.start()
+
     barrier = pltpu.get_barrier_semaphore()
     for side in (left, right):
         pl.semaphore_signal(barrier, inc=1, device_id={"cluster": side}, device_id_type=MESH)
@@ -76,6 +85,26 @@
     to_right, to_left = to_side(0, right), to_side(1, left)
     to_right.start()
     to_left.start()
+
+    ends = chain >= 4
+    pitch = chain - 1 if ends else 1
+    at_end = (here == 0) | (here == chain - 1)
+    inner = (here == 1) | (here == chain - 2)
+    inward = 1 + (here // pitch) * (chain - 3) if ends else here
+
+    def end_copy(k, source, where):
+        return pltpu.make_async_remote_copy(
+            src_ref=source, dst_ref=end_arrived.at[k], send_sem=end_send.at[k],
+            recv_sem=end_recv.at[k], device_id=where, device_id_type=MESH)
+
+    to_inner = end_copy(0, traces_ref, {"station": inward})
+    pass_right = end_copy(1, end_arrived.at[0], {"cluster": right})
+    pass_left = end_copy(2, end_arrived.at[0], {"cluster": left})
+
+    if ends:
+        @pl.when(at_end)
+        def _():
+            to_inner.start()
 
     def place(values, row, base, ref):
         for col in range(cols):
@@ -84,22 +113,36 @@
             flat = ref.reshape(ref.shape[0] * lines, LANES)
             flat[pl.ds(start, events, stride=lines), :] = values[:, col * LANES:(col + 1) * LANES]
 
-    def transform(source, base, also_weighted):
+    def transform(source, slot, spectra_to, weighted_to, station):
         group = 4 if rows % 4 == 0 else 1
         for first in range(0, rows, group):
             found = dot3(source[pl.ds(first * events, group * events), :], fh_ref[...], fl_ref[...])
             for k in range(group):
                 row = first + k
                 values = found[k * events:(k + 1) * events]
-                place(values, row, base * events, spectra)
-                if also_weighted:
-                    place(values * weight_ref[here * (rows // channels) + row // channels], row, 0, weighted)
-
-    transform(traces_ref, 0, True)
+                place(values, row, slot * events, spectra_to)
+                if weighted_to is not None:
+                    weight = weight_ref[station * (rows // channels) + row // channels]
+                    place(values * weight, row, 0, weighted_to)
+
+    spectra[3 * events] = jnp.zeros(spectra.shape[1:], jnp.float32)
+    end_spectra[3 * events] = jnp.zeros(spectra.shape[1:], jnp.float32)
+    tables[0].wait()
+    tables[1].wait()
+    transform(traces_ref, 0, spectra, weighted, here)
     to_left.wait()
-    transform(arrived.at[1], 2, False)
+    transform(arrived.at[1], 2, spectra, None, here)
     to_right.wait()
-    transform(arrived.at[0], 1, False)
+    if ends:
+        @pl.when(inner)
+        def _():
+            to_inner.wait_recv()
+            pass_right.start()
+            pass_left.start()
+
+    transform(arrived.at[0], 1, spectra, None, here)
+    tables[2].wait()
+    tables[3].wait()
 
     sub = lax.broadcasted_iota(jnp.int32, (8, LANES), 0)
     in_low4 = sub < 4
@@ -110,28 +153,37 @@
 
     deep = lines // 2
 
-    def one_pair(spot):
-        a = weighted[first_ref[spot]]
-        b = spectra[second_ref[spot]]
+    def one_pair(spot, turn_facts, left_rows, right_rows):
+        slot, own_count, other_count = turn_facts
+        first, second = pair_ref[2 * spot], pair_ref[2 * spot + 1]
+        valid = (first < own_count) & (second < other_count)
+        a = left_rows[first]
+        b = right_rows[jnp.where(valid, slot * events + second, 3 * events)]
         re_a, im_a, re_b, im_b = a[:deep], a[deep:], b[:deep], b[deep:]
         real = re_a * re_b + im_a * im_b
         imag = im_a * re_b - re_a * im_b
         return (sum(real[k:k + 8] for k in range(0, deep, 8)),
                 sum(imag[k:k + 8] for k in range(0, deep, 8)))
 
-    def fill(turn, dest):
+    def fill(turn, dest, left_rows, right_rows, add):
         base = (turn * chain + dest) * share
+        partner = partner_ref[turn * ring + cluster]
+        slot = jnp.where(partner == cluster, 0, jnp.where(partner == right, 2, 1))
+        turn_facts = (slot, count_ref[cluster], count_ref[partner])
 
         def body(step, carry):
             for k in range(0, 8, 2):
                 spot = base + step * 8 + k
-                real0, imag0 = one_pair(spot)
-                real1, imag1 = one_pair(spot + 1)
+                real0, imag0 = one_pair(spot, turn_facts, left_rows, right_rows)
+                real1, imag1 = one_pair(spot + 1, turn_facts, left_rows, right_rows)
                 reals = fold(real0, real1, in_low4, 4)
                 imags = fold(imag0, imag1, in_low4, 4)
                 both = jnp.where(in_low2, reals, imags) + jnp.where(
                     in_low2, pltpu.roll(reals, 6, 0), pltpu.roll(imags, 2, 0))
-                part[turn * chain + dest, pl.ds(pl.multiple_of(step * 32 + k * 4, 8), 8), :] = both
+                place_at = pl.ds(pl.multiple_of(step * 32 + k * 4, 8), 8)
+                if add:
+                    both = both + part[turn * chain + dest, place_at, :]
+                part[turn * chain + dest, place_at, :] = both
             return carry
 
         lax.fori_loop(0, share // 8, body, 0)
@@ -150,19 +202,30 @@
 
     far_first = sorted(range(chain), key=lambda d: -abs(2 * d - chain + 1))
 
+    def by_end(low, dest):
+        if not ends:
+            return False
+        return dest == 1 if low else dest == chain - 2
+
     def compute(turn):
         for dest in far_first:
-            fill(turn, dest)
-
-            @pl.when((here == 0) & (dest > here))
-            def _():
-                upward(turn, dest).start()
-
-            @pl.when((here == chain - 1) & (dest < here))
-            def _():
-                downward(turn, dest).start()
-
-    def forward(turn):
+            given = ((here == 0) & by_end(True, dest)) | ((here == chain - 1) & by_end(False, dest))
+
+            @pl.when(jnp.logical_not(given))
+            def _():
+                fill(turn, dest, weighted, spectra, False)
+
+            if not by_end(True, dest):
+                @pl.when((here == 0) & (dest > here))
+                def _():
+                    upward(turn, dest).start()
+
+            if not by_end(False, dest):
+                @pl.when((here == chain - 1) & (dest < here))
+                def _():
+                    downward(turn, dest).start()
+
+    def pass_up(turn):
         for dest in far_first:
             spot = turn * chain + dest
 
@@ -172,20 +235,57 @@
                 part[spot] = part[spot] + from_below[spot]
                 upward(turn, dest).start()
 
+    def pass_down(turn):
+        for dest in far_first:
+            spot = turn * chain + dest
+
             @pl.when((here < chain - 1) & (dest < here))
             def _():
                 downward(turn, dest).wait_recv()
                 part[spot] = part[spot] + from_above[spot]
                 downward(turn, dest).start()
 
+    lower = 2 * here < chain
+
+    def pass_near(turn):
+        @pl.when(lower)
+        def _():
+            pass_up(turn)
+
+        @pl.when(jnp.logical_not(lower))
+        def _():
+            pass_down(turn)
+
+    def pass_far(turn):
+        @pl.when(lower)
+        def _():
+            pass_down(turn)
+
+        @pl.when(jnp.logical_not(lower))
+        def _():
+            pass_up(turn)
+
+    gets_below = (here > 1) if ends else (here > 0)
+    gets_above = (here < chain - 2) if ends else (here < chain - 1)
+    weight_sum = weight_ref[0]
+    for k in range(1, weight_ref.shape[0]):
+        weight_sum = weight_sum + weight_ref[k]
+    scale = 1.0 / (channels * jnp.full((1, gh_ref.shape[1]), weight_sum, jnp.float32))
+
+    def final(turn):
         spot = turn * chain + here
 
-        @pl.when(here > 0)
+        if ends:
+            @pl.when(inner)
+            def _():
+                fill(turn, here, end_weighted, end_spectra, True)
+
+        @pl.when(gets_below)
         def _():
             upward(turn, here).wait_recv()
             part[spot] = part[spot] + from_below[spot]
 
-        @pl.when(here < chain - 1)
+        @pl.when(gets_above)
         def _():
             downward(turn, here).wait_recv()
             part[spot] = part[spot] + from_above[spot]
@@ -195,25 +295,58 @@
             piece = part[spot, pl.ds(col, share, stride=cols), :]
             table = pl.ds(col * LANES, LANES)
             total = total + dot3(piece, gh_ref[table, :], gl_ref[table, :])
-        out_ref[turn] = total * scale_ref[turn]
+        out_ref[turn] = total * scale
+
+    def end_phase():
+        if ends:
+            @pl.when(inner)
+            def _():
+                end_station = ((here - 1) // (chain - 3)) * (chain - 1)
+                transform(end_arrived.at[0], 0, end_spectra, end_weighted, end_station)
+                pass_left.wait()
+                transform(end_arrived.at[2], 2, end_spectra, None, end_station)
+                pass_right.wait()
+                transform(end_arrived.at[1], 1, end_spectra, None, end_station)
+
+            @pl.when(at_end)
+            def _():
+                to_inner.wait_send()
 
     compute(0)
 
     def turn_body(turn, carry):
-        compute(turn + 1)
-        forward(turn)
+        @pl.when(turn < rounds - 1)
+        def _():
+            compute(turn + 1)
+
+        pass_near(turn)
+
+        @pl.when(turn > 0)
+        def _():
+            pass_far(turn - 1)
+
+            @pl.when(turn == 1)
+            def _():
+                end_phase()
+
+            final(turn - 1)
+
         return carry
 
-    lax.fori_loop(0, rounds - 1, turn_body, 0)
-    forward(rounds - 1)
+    lax.fori_loop(0, rounds, turn_body, 0)
+    pass_far(rounds - 1)
+    final(rounds - 1)
 
     def drain(turn, carry):
         for dest in range(chain):
-            @pl.when(dest > here)
+            sent_up = (dest > here) & (here > 0) if by_end(True, dest) else dest > here
+            sent_down = (dest < here) & (here < chain - 1) if by_end(False, dest) else dest < here
+
+            @pl.when(sent_up)
             def _():
                 upward(turn, dest).wait_send()
 
-            @pl.when(dest < here)
+            @pl.when(sent_down)
             def _():
                 downward(turn, dest).wait_send()
         return carry
@@ -224,9 +357,7 @@
 def on_device(waveforms, event_mask, station_weight, partners, pair_list, counts):
     events, stations, channels, samples = waveforms.shape
     rounds, _, pairs, _ = pair_list.shape
-    cluster = lax.axis_index("cluster")
     ring = lax.axis_size("cluster")
-    here = lax.axis_index("station")
     chain = lax.axis_size("station")
     rows = stations * channels
     share = pairs // chain
@@ -237,37 +368,34 @@
     unit = waveforms * (lax.rsqrt(energy + epsilon) * event_mask[:, :, None, None].astype(jnp.float32))
     traces = jnp.transpose(unit, (1, 2, 0, 3)).reshape(rows * events, samples)
 
-    partner = partners[:, cluster]
-    slot = jnp.where(partner == cluster, 0, jnp.where(partner == (cluster + 1) % ring, 2, 1))
-    i, j = pair_list[:, 0, :, 0], pair_list[:, 0, :, 1]
-    first = i.reshape(-1)
-    second = (slot[:, None] * events + j).reshape(-1)
-    valid = ((i < counts[cluster]) & (j < counts[partner][:, None])).astype(jnp.float32)
-    scale = valid / (channels * jnp.sum(station_weight))
-    scale = lax.dynamic_slice_in_dim(scale, here * share, share, 1)[:, :, None]
-
     vmem = pl.BlockSpec(memory_space=pltpu.VMEM)
     smem = pl.BlockSpec(memory_space=pltpu.SMEM)
+    hbm = pl.BlockSpec(memory_space=pltpu.HBM)
+    lines = pltpu.VMEM((events, rows * cols, LANES), jnp.float32)
+    all_lines = pltpu.VMEM((3 * events + 1, rows * cols, LANES), jnp.float32)
     blocks = rounds * chain
     block = pltpu.VMEM((blocks, share * cols, LANES), jnp.float32)
     out = pl.pallas_call(
         functools.partial(kernel, (events, rows, rounds, chain, share, ring, channels)),
         out_shape=jax.ShapeDtypeStruct((rounds, share, 2 * samples), jnp.float32),
-        in_specs=[smem, smem, smem] + [vmem] * 6,
+        in_specs=[smem] * 4 + [vmem] + [hbm] * 4,
         out_specs=vmem,
         scratch_shapes=[
+            *(pltpu.VMEM(table.shape, jnp.bfloat16) for table in (fh, fl, gh, gl)),
             pltpu.VMEM((2, rows * events, samples), jnp.float32),
-            pltpu.VMEM((events, rows * cols, LANES), jnp.float32),
-            pltpu.VMEM((3 * events, rows * cols, LANES), jnp.float32),
+            pltpu.VMEM((3, rows * events, samples), jnp.float32),
+            lines, all_lines, lines, all_lines,
             block, block, block,
+            pltpu.SemaphoreType.DMA((4,)),
             pltpu.SemaphoreType.DMA((2,)), pltpu.SemaphoreType.DMA((2,)),
+            pltpu.SemaphoreType.DMA((3,)), pltpu.SemaphoreType.DMA((3,)),
             pltpu.SemaphoreType.DMA((blocks,)), pltpu.SemaphoreType.DMA((blocks,)),
             pltpu.SemaphoreType.DMA((blocks,)), pltpu.SemaphoreType.DMA((blocks,)),
         ],
         compiler_params=pltpu.CompilerParams(
-            collective_id=0, has_side_effects=True, vmem_limit_bytes=40 << 20),
+            collective_id=0, has_side_effects=True, vmem_limit_bytes=48 << 20),
         name="stack_pairs",
-    )(first, second, station_weight, traces, scale, fh, fl, gh, gl)
+    )(pair_list.reshape(-1), partners.reshape(-1), counts, station_weight, traces, fh, fl, gh, gl)
     return out[:, None]
 
 

time: 76.6 us -> 57.1 us (0.75)
  the two profiles are of different devices: /device:TPU:14 before, /device:TPU:0 now
where the time goes in v2:
time: 57.1 us; the launch traced here: 56.9 us
  Pallas kernels  51.1 us (89%)
  local copies, waits for them, and re-layouts  3.58 us (6%)
  other arithmetic  2.07 us (4%)
    pallas_call x1, Pallas kernels, on_device(): pl.pallas_call(functools.partial(kernel, (events, rows, rounds, chain, sh...  51.1 us
    unnamed x18, local copies, waits for them, and re-layouts  2.33 us
    reduce_sum x1, other arithmetic, on_device(): energy = jnp.sum(waveforms * waveforms, axis=-1, keepdims=True)  1.19 us

profile of v2, /device:TPU:0, one launch (start us, length us, event | category | flops | bytes accessed | tf_op | source)
XLA Modules:
  0.0 56.9 jit_solution(1768445664751249101)
XLA Ops:
  0.0 0.0 copy-start.6
  0.0 0.8 %reshape.22.partner_ref = s32[16]{0:T(128)S(1)} reshape(s32[4,4]{1,0:T(4,128)} %param.13) | data formatting | bytes 128 | tf_op jit(solution)/shard_map/reshape | solution.py:398
  0.8 0.7 %convert_element_type.4 = f32[32,4]{0,1:T(4,128)S(1)} convert(s32[32,4]{0,1:T(4,128)} %param.11) | non-fusion elementwise | flops 128 | bytes 1024 | tf_op jit(solution)/shard_map/convert_element_type | solution.py:368
  1.5 0.1 copy.15
  1.6 1.2 %multiply_reduce_fusion = f32[32,4,3]{1,2,0:T(4,128)S(1)} fusion(f32[32,4,3,256]{3,1,2,0:T(4,128)} %param.10), kind=kLoop, calls=%fused_computation.1 | loop fusion | flops 196224 | bytes 394752 | tf_op jit(solution)/shard_map/reduce_sum | solution.py:367
  2.8 0.0 copy-done.6
  2.8 0.2 multiply_bitcast_fusion
  3.0 0.0 copy-start.7
  3.0 0.0 copy-start.2
  3.0 0.0 copy-start.3
  3.0 0.1 copy.16
  3.1 0.6 %copy-done.7 = s32[4,1,256,2]{2,3,1,0:T(2,128)S(1)} copy-done((s32[4,1,256,2]{2,3,1,0:T(2,128)S(1)}, s32[4,1,256,2]{2,3,1,0:T(2,128)}, u32[]{:S(2)}) %copy-start.7) | copy-done | bytes 8216
  3.7 0.0 copy-start
  3.7 0.0 copy-start.1
  3.7 0.2 copy.14
  3.9 0.0 copy-start.4
  4.0 0.0 copy-start.5
  4.0 0.3 reshape.21.pair_ref
  4.2 0.0 copy-done.2
  4.2 0.0 copy-done.3
  4.2 0.5 copy-done
  4.8 0.2 copy-done.1
  5.0 0.0 copy-done.4
  5.0 0.0 copy-done.5
  5.0 51.1 %stack_pairs.1 = f32[4,64,512]{2,1,0:T(8,128)S(1)} custom-call(s32[2048]{0:T(1024)S(1)} %reshape.21.pair_ref, s32[16]{0:T(128)S(1)} %reshape.22.partner_ref, s32[4]{0:T(128)S(1)} %copy-done.4, f32[16]{0:T(128)S(1)} %copy-done.5, f32[384,256]{1,0:T(8,128)S(1)} %bitcast.11, bf16[256,512]{1,0:T(8,128)(2,1)S(1)} %copy-done.3, bf16[256,512]{1,0:T(8,128)(2,1)S(1)} %copy-done.2, ...), custom_call_target="tpu_custom_call" | custom-call | tf_op jit(solution)/shard_map/stack_pairs/pallas_call | solution.py:378
  56.1 0.8 %copy.19 = f32[4,1,64,512]{3,2,1,0:T(8,128)} copy(f32[4,1,64,512]{3,2,1,0:T(8,128)S(1)} %bitcast.10) | data formatting | bytes 1048576
  (1 shorter events, 0.0 us)
Async XLA Ops:
  0.0 2.8 %copy-start.6 = (f32[32,4,3,256]{3,1,2,0:T(4,128)S(1)}, f32[32,4,3,256]{3,1,2,0:T(4,128)}, u32[]{:S(2)}) copy-start(f32[32,4,3,256]{3,1,2,0:T(4,128)} %param.10) | copy-start | bytes 1179652
  3.0 0.7 %copy-start.7 = (s32[4,1,256,2]{2,3,1,0:T(2,128)S(1)}, s32[4,1,256,2]{2,3,1,0:T(2,128)}, u32[]{:S(2)}) copy-start(s32[4,1,256,2]{2,3,1,0:T(2,128)} %param.14) | copy-start | bytes 24580
  3.0 1.2 %copy-start.2 = (bf16[256,512]{1,0:T(8,128)(2,1)S(1)}, bf16[256,512]{1,0:T(8,128)(2,1)}, u32[]{:S(2)}) copy-start(bf16[256,512]{1,0:T(8,128)(2,1)} %constant.13.clone.fl_hbm) | copy-start | bytes 786436
  3.0 1.2 %copy-start.3 = (bf16[256,512]{1,0:T(8,128)(2,1)S(1)}, bf16[256,512]{1,0:T(8,128)(2,1)}, u32[]{:S(2)}) copy-start(bf16[256,512]{1,0:T(8,128)(2,1)} %constant.12.clone.fh_hbm) | copy-start | bytes 786436
  3.7 1.1 %copy-start = (bf16[512,512]{1,0:T(8,128)(2,1)S(1)}, bf16[512,512]{1,0:T(8,128)(2,1)}, u32[]{:S(2)}) copy-start(bf16[512,512]{1,0:T(8,128)(2,1)} %constant.15.clone.gl_hbm) | copy-start | bytes 1572868
  3.7 1.2 %copy-start.1 = (bf16[512,512]{1,0:T(8,128)(2,1)S(1)}, bf16[512,512]{1,0:T(8,128)(2,1)}, u32[]{:S(2)}) copy-start(bf16[512,512]{1,0:T(8,128)(2,1)} %constant.14.clone.gh_hbm) | copy-start | bytes 1572868
  3.9 1.0 %copy-start.4 = (s32[4]{0:T(128)S(1)}, s32[4]{0:T(128)}, u32[]{:S(2)}) copy-start(s32[4]{0:T(128)} %count_ref.1) | copy-start | bytes 52
  4.0 1.0 %copy-start.5 = (f32[16]{0:T(128)S(1)}, f32[16]{0:T(128)}, u32[]{:S(2)}) copy-start(f32[16]{0:T(128)} %weight_ref.1) | copy-start | bytes 196

commit v3 on v2

--- a/solution.py
+++ b/solution.py
@@ -116,7 +116,9 @@
     def transform(source, slot, spectra_to, weighted_to, station):
         group = 4 if rows % 4 == 0 else 1
         for first in range(0, rows, group):
-            found = dot3(source[pl.ds(first * events, group * events), :], fh_ref[...], fl_ref[...])
+            found = source[pl.ds(first * events, group * events), :]
+            found = found * lax.rsqrt(jnp.sum(found * found, axis=-1, keepdims=True) + epsilon)
+            found = dot3(found, fh_ref[...], fl_ref[...])
             for k in range(group):
                 row = first + k
                 values = found[k * events:(k + 1) * events]
@@ -167,7 +169,7 @@
 
     def fill(turn, dest, left_rows, right_rows, add):
         base = (turn * chain + dest) * share
-        partner = partner_ref[turn * ring + cluster]
+        partner = partner_ref[turn, cluster]
         slot = jnp.where(partner == cluster, 0, jnp.where(partner == right, 2, 1))
         turn_facts = (slot, count_ref[cluster], count_ref[partner])
 
@@ -364,9 +366,8 @@
     cols = 2 * samples // LANES
     fh, fl, gh, gl = make_tables(samples)
 
-    energy = jnp.sum(waveforms * waveforms, axis=-1, keepdims=True)
-    unit = waveforms * (lax.rsqrt(energy + epsilon) * event_mask[:, :, None, None].astype(jnp.float32))
-    traces = jnp.transpose(unit, (1, 2, 0, 3)).reshape(rows * events, samples)
+    masked = waveforms * event_mask[:, :, None, None].astype(jnp.float32)
+    traces = jnp.transpose(masked, (1, 2, 0, 3)).reshape(rows * events, samples)
 
     vmem = pl.BlockSpec(memory_space=pltpu.VMEM)
     smem = pl.BlockSpec(memory_space=pltpu.SMEM)
@@ -395,7 +396,7 @@
         compiler_params=pltpu.CompilerParams(
             collective_id=0, has_side_effects=True, vmem_limit_bytes=48 << 20),
         name="stack_pairs",
-    )(pair_list.reshape(-1), partners.reshape(-1), counts, station_weight, traces, fh, fl, gh, gl)
+    )(pair_list.reshape(-1), partners, counts, station_weight, traces, fh, fl, gh, gl)
     return out[:, None]
 
 

time: 57.1 us -> 56.5 us (0.989)
  local copies, waits for them, and re-layouts: 3.58 us -> 2.75 us
    reduce_sum x1 -> x0, other arithmetic: 1.19 us -> none  [on_device(): energy = jnp.sum(waveforms * waveforms, axis=-1, keepdims=True)]
    transpose x1, other arithmetic: 0.17 us -> 1.12 us  [on_device(): traces = jnp.transpose(masked, (1, 2, 0, 3)).reshape(rows * events, samples)]
    reshape x1 -> x0, local copies, waits for them, and re-layouts: 0.81 us -> none  [on_device(): partners.reshape(-1)]
where the time goes in v3:
time: 56.5 us; the launch traced here: 56.3 us
  Pallas kernels  51.6 us (91%)
  local copies, waits for them, and re-layouts  2.75 us (5%)
  other arithmetic  1.8 us (3%)
    pallas_call x1, Pallas kernels, on_device(): pl.pallas_call(functools.partial(kernel, (events, rows, rounds, chain, sh...  51.6 us
    unnamed x18, local copies, waits for them, and re-layouts  2.32 us

profile of v3, /device:TPU:0, one launch (start us, length us, event | category | flops | bytes accessed | tf_op | source)
XLA Modules:
  0.0 56.3 jit_solution(11077108617004156163)
XLA Ops:
  0.0 0.7 %convert_element_type.4 = f32[32,4]{0,1:T(4,128)S(1)} convert(s32[32,4]{0,1:T(4,128)} %param.11) | non-fusion elementwise | flops 128 | bytes 1024 | tf_op jit(solution)/shard_map/convert_element_type | solution.py:369
  0.7 0.1 copy.15
  0.8 1.1 %multiply_bitcast_fusion = f32[4,3,32,256]{3,0,1,2:T(4,128)S(1)} fusion(f32[32,4,3,256]{3,1,2,0:T(4,128)} %param.10, f32[32,4]{1,0:T(8,128)S(1)} %copy.15), kind=kLoop, calls=%fused_computation | loop fusion | flops 98304 | bytes 786944 | tf_op jit(solution)/shard_map/transpose | solution.py:370
  1.9 0.0 copy-start.7
  1.9 0.0 copy-start.2
  1.9 0.0 copy-start.3
  1.9 0.1 copy.16
  2.0 0.6 %copy-done.7 = s32[4,1,256,2]{2,3,1,0:T(2,128)S(1)} copy-done((s32[4,1,256,2]{2,3,1,0:T(2,128)S(1)}, s32[4,1,256,2]{2,3,1,0:T(2,128)}, u32[]{:S(2)}) %copy-start.7) | copy-done | bytes 8216
  2.6 0.0 copy-start
  2.6 0.0 copy-start.1
  2.6 0.2 copy.14
  2.8 0.0 copy-start.4
  2.8 0.0 copy-start.5
  2.9 0.0 copy-start.6
  2.9 0.3 reshape.8.pair_ref
  3.1 0.0 copy-done.2
  3.1 0.0 copy-done.3
  3.2 0.5 copy-done
  3.7 0.2 copy-done.1
  3.8 0.0 copy-done.4
  3.8 0.0 copy-done.5
  3.8 0.0 copy-done.6
  3.9 51.6 %stack_pairs.1 = f32[4,64,512]{2,1,0:T(8,128)S(1)} custom-call(s32[2048]{0:T(1024)S(1)} %reshape.8.pair_ref, s32[4,4]{1,0:T(4,128)S(1)} %copy-done.4, s32[4]{0:T(128)S(1)} %copy-done.5, f32[16]{0:T(128)S(1)} %copy-done.6, f32[384,256]{1,0:T(8,128)S(1)} %bitcast.11, bf16[256,512]{1,0:T(8,128)(2,1)S(1)} %copy-done.3, bf16[256,512]{1,0:T(8,128)(2,1)S(1)} %copy-done.2, ...), custom_call_target="tpu_custom_call" | custom-call | tf_op jit(solution)/shard_map/stack_pairs/pallas_call | solution.py:379
  55.5 0.8 %copy.19 = f32[4,1,64,512]{3,2,1,0:T(8,128)} copy(f32[4,1,64,512]{3,2,1,0:T(8,128)S(1)} %bitcast.10) | data formatting | bytes 1048576
Async XLA Ops:
  1.9 0.7 %copy-start.7 = (s32[4,1,256,2]{2,3,1,0:T(2,128)S(1)}, s32[4,1,256,2]{2,3,1,0:T(2,128)}, u32[]{:S(2)}) copy-start(s32[4,1,256,2]{2,3,1,0:T(2,128)} %param.14) | copy-start | bytes 24580
  1.9 1.2 %copy-start.2 = (bf16[256,512]{1,0:T(8,128)(2,1)S(1)}, bf16[256,512]{1,0:T(8,128)(2,1)}, u32[]{:S(2)}) copy-start(bf16[256,512]{1,0:T(8,128)(2,1)} %constant.9.clone.fl_hbm) | copy-start | bytes 786436
  1.9 1.2 %copy-start.3 = (bf16[256,512]{1,0:T(8,128)(2,1)S(1)}, bf16[256,512]{1,0:T(8,128)(2,1)}, u32[]{:S(2)}) copy-start(bf16[256,512]{1,0:T(8,128)(2,1)} %constant.8.clone.fh_hbm) | copy-start | bytes 786436
  2.6 1.1 %copy-start = (bf16[512,512]{1,0:T(8,128)(2,1)S(1)}, bf16[512,512]{1,0:T(8,128)(2,1)}, u32[]{:S(2)}) copy-start(bf16[512,512]{1,0:T(8,128)(2,1)} %constant.11.clone.gl_hbm) | copy-start | bytes 1572868
  2.6 1.2 %copy-start.1 = (bf16[512,512]{1,0:T(8,128)(2,1)S(1)}, bf16[512,512]{1,0:T(8,128)(2,1)}, u32[]{:S(2)}) copy-start(bf16[512,512]{1,0:T(8,128)(2,1)} %constant.10.clone.gh_hbm) | copy-start | bytes 1572868
  2.8 1.0 %copy-start.4 = (s32[4,4]{1,0:T(4,128)S(1)}, s32[4,4]{1,0:T(4,128)}, u32[]{:S(2)}) copy-start(s32[4,4]{1,0:T(4,128)} %partner_ref.1) | copy-start | bytes 196
  2.8 1.0 %copy-start.5 = (s32[4]{0:T(128)S(1)}, s32[4]{0:T(128)}, u32[]{:S(2)}) copy-start(s32[4]{0:T(128)} %count_ref.1) | copy-start | bytes 52
  2.9 1.0 %copy-start.6 = (f32[16]{0:T(128)S(1)}, f32[16]{0:T(128)}, u32[]{:S(2)}) copy-start(f32[16]{0:T(128)} %weight_ref.1) | copy-start | bytes 196

commit v4 on v3

--- a/solution.py
+++ b/solution.py
@@ -156,8 +156,8 @@
     deep = lines // 2
 
     def one_pair(spot, turn_facts, left_rows, right_rows):
-        slot, own_count, other_count = turn_facts
-        first, second = pair_ref[2 * spot], pair_ref[2 * spot + 1]
+        offset, slot, own_count, other_count = turn_facts
+        first, second = pair_ref[spot + offset], pair_ref[spot + offset + chain * share]
         valid = (first < own_count) & (second < other_count)
         a = left_rows[first]
         b = right_rows[jnp.where(valid, slot * events + second, 3 * events)]
@@ -171,7 +171,7 @@
         base = (turn * chain + dest) * share
         partner = partner_ref[turn, cluster]
         slot = jnp.where(partner == cluster, 0, jnp.where(partner == right, 2, 1))
-        turn_facts = (slot, count_ref[cluster], count_ref[partner])
+        turn_facts = (turn * chain * share, slot, count_ref[cluster], count_ref[partner])
 
         def body(step, carry):
             for k in range(0, 8, 2):
@@ -396,7 +396,7 @@
         compiler_params=pltpu.CompilerParams(
             collective_id=0, has_side_effects=True, vmem_limit_bytes=48 << 20),
         name="stack_pairs",
-    )(pair_list.reshape(-1), partners, counts, station_weight, traces, fh, fl, gh, gl)
+    )(jnp.transpose(pair_list, (0, 1, 3, 2)).reshape(-1), partners, counts, station_weight, traces, fh, fl, gh, gl)
     return out[:, None]
 
 

time: 56.5 us -> 56.4 us (level)
    unnamed x18 -> x16, local copies, waits for them, and re-layouts: 2.32 us -> 2.48 us
where the time goes in v4:
time: 56.4 us; the launch traced here: 56.2 us
  Pallas kernels  51.6 us (91%)
  local copies, waits for them, and re-layouts  2.64 us (5%)
  other arithmetic  1.88 us (3%)
    pallas_call x1, Pallas kernels, on_device(): pl.pallas_call(functools.partial(kernel, (events, rows, rounds, chain, sh...  51.6 us
    unnamed x16, local copies, waits for them, and re-layouts  2.48 us
    transpose x1, other arithmetic, on_device(): traces = jnp.transpose(masked, (1, 2, 0, 3)).reshape(rows * events, samples)  1.2 us

profile of v4, /device:TPU:0, one launch (start us, length us, event | category | flops | bytes accessed | tf_op | source)
XLA Modules:
  0.0 56.2 jit_solution(1724077765727696862)
XLA Ops:
  0.0 0.7 %convert_element_type.4 = f32[32,4]{0,1:T(4,128)S(1)} convert(s32[32,4]{0,1:T(4,128)} %param.11) | non-fusion elementwise | flops 128 | bytes 1024 | tf_op jit(solution)/shard_map/convert_element_type | solution.py:369
  0.7 0.7 %copy.14 = s32[4,2,2,128]{3,1,2,0:T(2,128)S(1)} copy(s32[4,2,2,128]{3,2,1,0:T(2,128)} %bitcast.12) | data formatting | bytes 16384
  1.4 0.1 copy.11
  1.5 0.0 copy-start.1
  1.5 0.0 copy-start.3
  1.5 0.0 copy-start.4
  1.5 1.2 %multiply_bitcast_fusion = f32[4,3,32,256]{3,0,1,2:T(4,128)S(1)} fusion(f32[32,4,3,256]{3,1,2,0:T(4,128)} %param.10, f32[32,4]{1,0:T(8,128)S(1)} %copy.11), kind=kLoop, calls=%fused_computation | loop fusion | flops 98304 | bytes 786944 | tf_op jit(solution)/shard_map/transpose | solution.py:370
  2.7 0.0 copy-start
  2.7 0.0 copy-start.2
  2.7 0.1 copy.12
  2.8 0.0 copy-start.5
  2.8 0.0 copy-start.6
  2.8 0.0 copy-done.1
  2.8 0.0 copy-done.3
  2.8 0.0 copy-done.4
  2.8 0.9 %copy-done = bf16[512,512]{1,0:T(8,128)(2,1)S(1)} copy-done((bf16[512,512]{1,0:T(8,128)(2,1)S(1)}, bf16[512,512]{1,0:T(8,128)(2,1)}, u32[]{:S(2)}) %copy-start) | copy-done | bytes 524312
  3.7 0.1 copy-done.2
  3.8 0.0 copy-done.5
  3.8 0.0 copy-done.6
  3.8 51.6 %stack_pairs.1 = f32[4,64,512]{2,1,0:T(8,128)S(1)} custom-call(s32[2048]{0:T(1024)S(1)} %bitcast.11, s32[4,4]{1,0:T(4,128)S(1)} %copy-done.4, s32[4]{0:T(128)S(1)} %copy-done.5, f32[16]{0:T(128)S(1)} %copy-done.6, f32[384,256]{1,0:T(8,128)S(1)} %bitcast.10, bf16[256,512]{1,0:T(8,128)(2,1)S(1)} %copy-done.3, bf16[256,512]{1,0:T(8,128)(2,1)S(1)} %copy-done.2, ...), custom_call_target="tpu_custom_call" | custom-call | tf_op jit(solution)/shard_map/stack_pairs/pallas_call | solution.py:379
  55.4 0.8 %copy.16 = f32[4,1,64,512]{3,2,1,0:T(8,128)} copy(f32[4,1,64,512]{3,2,1,0:T(8,128)S(1)} %bitcast.9) | data formatting | bytes 1048576
Async XLA Ops:
  1.5 1.3 %copy-start.1 = (bf16[512,512]{1,0:T(8,128)(2,1)S(1)}, bf16[512,512]{1,0:T(8,128)(2,1)}, u32[]{:S(2)}) copy-start(bf16[512,512]{1,0:T(8,128)(2,1)} %constant.10.clone.gh_hbm) | copy-start | bytes 1572868
  1.5 1.4 %copy-start.3 = (bf16[256,512]{1,0:T(8,128)(2,1)S(1)}, bf16[256,512]{1,0:T(8,128)(2,1)}, u32[]{:S(2)}) copy-start(bf16[256,512]{1,0:T(8,128)(2,1)} %constant.8.clone.fh_hbm) | copy-start | bytes 786436
  1.5 1.4 %copy-start.4 = (s32[4,4]{1,0:T(4,128)S(1)}, s32[4,4]{1,0:T(4,128)}, u32[]{:S(2)}) copy-start(s32[4,4]{1,0:T(4,128)} %partner_ref.1) | copy-start | bytes 196
  2.7 1.0 %copy-start = (bf16[512,512]{1,0:T(8,128)(2,1)S(1)}, bf16[512,512]{1,0:T(8,128)(2,1)}, u32[]{:S(2)}) copy-start(bf16[512,512]{1,0:T(8,128)(2,1)} %constant.11.clone.gl_hbm) | copy-start | bytes 1572868
  2.7 1.1 %copy-start.2 = (bf16[256,512]{1,0:T(8,128)(2,1)S(1)}, bf16[256,512]{1,0:T(8,128)(2,1)}, u32[]{:S(2)}) copy-start(bf16[256,512]{1,0:T(8,128)(2,1)} %constant.9.clone.fl_hbm) | copy-start | bytes 786436
  2.8 1.0 %copy-start.5 = (s32[4]{0:T(128)S(1)}, s32[4]{0:T(128)}, u32[]{:S(2)}) copy-start(s32[4]{0:T(128)} %count_ref.1) | copy-start | bytes 52
  2.8 1.0 %copy-start.6 = (f32[16]{0:T(128)S(1)}, f32[16]{0:T(128)}, u32[]{:S(2)}) copy-start(f32[16]{0:T(128)} %weight_ref.1) | copy-start | bytes 196
